TPU v7x, 256 devices: a whole 4x4x8 slice. The times are simulated.
256 devices in a mesh: doc: 64 (over z, y, core), feat: 4 (over x).
Axes of the slice: x: 4, y: 4, z: 8, core: 2. Of those that a mesh axis runs over, the one named last changes fastest.
Arguments:
- scores: float32 [768, 128], P('doc'), may hold values from -6 to 6
- clicks: int32 [768, 128], P('doc'), may hold values from 0 to 1, as said below
- lengths: int32 [768], P('doc'), may hold values from 2 to 128, as said below
- t_plus_old: float32 [128], replicated, may hold values from 0.1 to 1
- t_minus_old: float32 [128], replicated, may hold values from 0.1 to 1
- leaf: int32 [98304], P('doc'), may hold values from 0 to 31
- bins: int32 [512, 98304], P('feat', 'doc'), may hold values from 0 to 255
Outputs:
- t_plus: float32 [128], replicated
- t_minus: float32 [128], replicated
- gradients: float32 [2, 98304], P(None, 'doc')
- hist: float32 [512, 64, 256], P(('feat', 'doc'))
Inputs may be any that keep to these rules, and one draw needn't show every extreme that they name: Query q shows its first lengths[q] slots; the first two queries of each block of 12 queries show all 128. `clicks`: values at or beyond a query's length carry no meaning. In the first query of each block of 12 queries the even positions are clicked and the odd ones not; in the second the reverse.
All inputs are finite; a program needn't handle non-finite values.
Results may differ from a plain program's by a relative error of at most 0.0024.
Values may be sent and summed in bfloat16 or wider, within the bound.
No kernel may reach another device: no remote copies, remote signals or barrier semaphores. Data moves between devices by JAX's collectives and lax.ppermute only.
A program may use at most 64 MiB of HBM per device.

v0:
```python
import jax
import jax.numpy as jnp
from jax import lax
from jax.sharding import PartitionSpec as P

BINS = 256
LEAVES = 32


def pair_terms(scores, clicks, lengths, t_plus_old, t_minus_old):
    npos = scores.shape[1]
    places = jnp.arange(npos)
    shown_mask = places[None, :] < lengths[:, None]
    clicked = jnp.where((clicks == 1) & shown_mask, 1.0, 0.0).astype(jnp.float32)
    skipped = jnp.where((clicks == 0) & shown_mask, 1.0, 0.0).astype(jnp.float32)
    paired = clicked[:, :, None] * skipped[:, None, :]
    discount = 1.0 / jnp.log2(2.0 + places.astype(jnp.float32))
    clicks_count = jnp.sum(clicked, axis=1)
    ideal_gain = jnp.sum(
        jnp.where(
            places[None, :].astype(jnp.float32) < clicks_count[:, None], discount[None, :], 0.0
        ),
        axis=1,
    )
    ideal_gain = jnp.maximum(ideal_gain, 1.0)
    change = (
        paired * jnp.abs(discount[:, None] - discount[None, :])[None] / ideal_gain[:, None, None]
    )
    spread = scores[:, :, None] - scores[:, None, :]
    weighted = change * jax.nn.softplus(-spread)
    plus_part = jnp.sum(weighted / t_minus_old[None, None, :], axis=(0, 2))
    minus_part = jnp.sum(weighted / t_plus_old[None, :, None], axis=(0, 1))
    return (change, spread, plus_part, minus_part)


def lambda_rows(change, spread, plus_sum, minus_sum):
    t_plus = jnp.sqrt(plus_sum / plus_sum[0])
    t_minus = jnp.sqrt(minus_sum / minus_sum[0])
    scaled = change / (t_plus[None, :, None] * t_minus[None, None, :])
    chance = jax.nn.sigmoid(-spread)
    lambda_pair = scaled * chance
    second = lambda_pair * (1.0 - chance)
    slopes = jnp.sum(lambda_pair, axis=1) - jnp.sum(lambda_pair, axis=2)
    curvature = jnp.sum(second, axis=1) + jnp.sum(second, axis=2)
    own_rows = jnp.stack([slopes.reshape(-1), curvature.reshape(-1)])
    return (t_plus, t_minus, own_rows)


def leaf_weights(slope_row, curve_row, leaf_row):
    leaf_hit = (leaf_row[None, :] == jnp.arange(LEAVES)[:, None]).astype(jnp.bfloat16)
    return jnp.concatenate([leaf_hit * slope_row[None, :], leaf_hit * curve_row[None, :]], axis=0)


def block_hist(bin_rows, weights, levels):
    one_hot = (bin_rows[:, None, :] == levels[None, :, None]).astype(jnp.bfloat16)
    return jnp.einsum("gr,nbr->ngb", weights, one_hot, preferred_element_type=jnp.float32)


def feature_hist(bin_rows, weights):
    levels = jnp.arange(BINS, dtype=jnp.int32)
    row_count = bin_rows.shape[0]
    block_size = 1
    for option in (8, 4, 2):
        if block_size == 1 and row_count % option == 0:
            block_size = option

    def one_block(block):
        return block_hist(block, weights, levels)

    stacked = lax.map(
        one_block, bin_rows.reshape(row_count // block_size, block_size, bin_rows.shape[1])
    )
    return stacked.reshape(row_count, weights.shape[0], BINS)


def body(scores, clicks, lengths, t_plus_old, t_minus_old, leaf, bins):
    per_feat = scores.shape[0] // lax.axis_size("feat")
    start_row = lax.axis_index("feat") * per_feat
    my_scores = lax.dynamic_slice_in_dim(scores, start_row, per_feat, 0)
    my_clicks = lax.dynamic_slice_in_dim(clicks, start_row, per_feat, 0)
    my_lengths = lax.dynamic_slice_in_dim(lengths, start_row, per_feat, 0)
    change, spread, plus_part, minus_part = pair_terms(
        my_scores, my_clicks, my_lengths, t_plus_old, t_minus_old
    )
    plus_sum, minus_sum = lax.psum((plus_part, minus_part), ("doc", "feat"))
    t_plus, t_minus, own_rows = lambda_rows(change, spread, plus_sum, minus_sum)
    gradients = lax.all_gather(own_rows, "feat", axis=1, tiled=True)
    rounded = gradients.astype(jnp.bfloat16)
    weights = leaf_weights(rounded[0], rounded[1], leaf)
    hist = lax.psum_scatter(feature_hist(bins, weights), "doc", scatter_dimension=0, tiled=True)
    return (t_plus, t_minus, gradients, hist)


def solution(mesh):
    placed = (P("doc", None), P("doc", None), P("doc"), P(), P(), P("doc"), P("feat", "doc"))
    return jax.shard_map(
        body,
        mesh=mesh,
        in_specs=placed,
        out_specs=(P(), P(), P(None, "doc"), P(("feat", "doc"), None, None)),
        check_vma=False,
    )
```

profile of v0, /device:TPU:2, one launch (start us, length us, event | category | flops | bytes accessed | tf_op | source)
XLA Modules:
  0.0 321.2 jit_solution(5064826501937953063)
XLA Ops:
  8.1 0.9 fusion.26
  9.2 1.0 divide_reduce_fusion
  10.2 78.7 %all-reduce = (f32[128]{0:T(128)S(1)}, f32[128]{0:T(128)S(1)}) all-reduce(f32[128]{0:T(128)S(1)} %get-tuple-element.47, f32[128]{0:T(128)S(1)} %get-tuple-element.46), channel_id=1, replica_groups=mesh['doc'=64,'feat'=4] {'doc','feat'}, use_global_device_ids=true, to_apply=%region_3.4 | all-reduce | flops 256 | bytes 2048 | tf_op jit(solution)/shard_map/psum | solution.py:85
  89.4 12.0 %all_gather.3 = f32[2,1536]{1,0:T(2,128)S(1)} all-gather(f32[2,384]{1,0:T(2,128)S(1)} %pad_maximum_fusion.1), channel_id=1, replica_groups=mesh['doc'=64,'feat'=4] {'feat'}, dimensions={1}, use_global_device_ids=true | all-gather | bytes 15360 | tf_op jit(solution)/shard_map/all_gather | solution.py:87
  102.3 61.6 %while.11 = (s32[]{:T(128)}, f32[16,8,64,256]{3,2,1,0:T(8,128)}, s32[16,8,1536]{2,1,0:T(8,128)}, bf16[64,1536]{1,0:T(8,128)(2,1)S(1)}, s32[]{:T(128)}) while((s32[]{:T(128)}, f32[16,8,64,256]{3,2,1,0:T(8,128)}, s32[16,8,1536]{2,1,0:T(8,128)}, bf16[64,1536]{1,0:T(8,128)(2,1)S(1)}, s32[]{:T(128)}) %tuple.41), condition=%wide.region_11.12_spmd.clone, body=%wide.region_10.11_spmd.clone.sunk | while | flops 405798912 | bytes 868929 | solution.py:70
  102.3 0.8 dynamic-slice_bitcast_fusion.2
  103.1 3.0 fusion.31
  106.1 0.8 dynamic-slice_bitcast_fusion.2
  106.9 3.1 fusion.31
  110.0 0.8 dynamic-slice_bitcast_fusion.2
  110.8 3.1 fusion.31
  113.8 0.8 dynamic-slice_bitcast_fusion.2
  114.7 3.1 fusion.31
  117.7 0.8 dynamic-slice_bitcast_fusion.2
  118.5 3.0 fusion.31
  121.5 0.8 dynamic-slice_bitcast_fusion.2
  122.3 3.1 fusion.31
  125.4 0.8 dynamic-slice_bitcast_fusion.2
  126.2 3.0 fusion.31
  129.2 0.8 dynamic-slice_bitcast_fusion.2
  130.0 3.1 fusion.31
  133.1 0.8 dynamic-slice_bitcast_fusion.2
  133.9 3.0 fusion.31
  136.9 0.8 dynamic-slice_bitcast_fusion.2
  137.7 3.1 fusion.31
  141.6 3.0 fusion.31
  145.4 3.1 fusion.31
  149.3 3.0 fusion.31
  153.1 3.1 fusion.31
  157.0 3.0 fusion.31
  160.8 3.1 fusion.31
  163.9 149.9 %reduce-scatter.2.cloned.1.call-done = f32[2,64,256]{2,1,0:T(8,128)} async-done(((f32[128,64,256]{2,1,0:T(8,128)}), f32[2,64,256]{2,1,0:T(8,128)}) %reduce-scatter.2.cloned.1.call-update) | async-done | bytes 131088 | tf_op jit(solution)/shard_map/reduce_scatter | solution.py:90
  (33 shorter events, 7.8 us)
Async XLA Ops:
  7.2 306.6 %reduce-scatter.2.cloned.1.call-start = ((), (), s32[]{:S(2)}) async-start(), calls=%async_computation.1 | async-start | bytes 8519680 | tf_op jit(solution)/shard_map/reduce_scatter | solution.py:90
  88.9 13.4 %copy-start = (f32[128]{0:T(128)}, f32[128]{0:T(128)S(1)}, u32[]{:S(2)}) copy-start(f32[128]{0:T(128)S(1)} %divide_sqrt_fusion) | copy-start | bytes 1540
  88.9 13.3 %copy-start.1 = (f32[128]{0:T(128)}, f32[128]{0:T(128)S(1)}, u32[]{:S(2)}) copy-start(f32[128]{0:T(128)S(1)} %divide_sqrt_fusion.1) | copy-start | bytes 1540
Sparse Core Ops, SparseCore 0:
  164.0 149.6 reduce-scatter.1
where the time goes:
time: 322 us; the launch traced here: 321 us
  waiting for transfers between devices  150 us (47%)
  blocking collectives  90.7 us (28%)
  matrix products  48.7 us (15%)
  local copies, waits for them, and re-layouts  14.2 us (4%)
  between operations  14.2 us (4%)
  other arithmetic  3.45 us (1%)
    reduce_scatter x1, waiting for transfers between devices, body(): lax.psum_scatter(feature_hist(bins, weights), 'doc', scatter_dimension=0,...  150 us
    psum x1, blocking collectives, body(): plus_sum, minus_sum = lax.psum((plus_part, minus_part), ('doc', 'feat'))  78.7 us
    dot_general x16, matrix products, block_hist(): jnp.einsum('gr,nbr->ngb', weights, one_hot, preferred_element_type=jnp.fl...  48.7 us
    eq x16, local copies, waits for them, and re-layouts, block_hist(): bin_rows[:, None, :] == levels[None, :, None]  12.8 us
    all_gather x1, blocking collectives, body(): gradients = lax.all_gather(own_rows, 'feat', axis=1, tiled=True)  12 us
  transfers between devices with their start and end apart: 1, of which 1 were waited for; matrix products, arithmetic and copies ran while one was open for 0% of the time, Pallas kernels for 0%

commit v1 on v0

--- a/solution.py
+++ b/solution.py
@@ -82,7 +82,7 @@
     change, spread, plus_part, minus_part = pair_terms(
         my_scores, my_clicks, my_lengths, t_plus_old, t_minus_old
     )
-    plus_sum, minus_sum = lax.psum((plus_part, minus_part), ("doc", "feat"))
+    plus_sum, minus_sum = lax.psum(lax.psum((plus_part, minus_part), "doc"), "feat")
     t_plus, t_minus, own_rows = lambda_rows(change, spread, plus_sum, minus_sum)
     gradients = lax.all_gather(own_rows, "feat", axis=1, tiled=True)
     rounded = gradients.astype(jnp.bfloat16)

time: 322 us -> 382 us (1.19)
  blocking collectives: 90.7 us -> 152 us
    psum x1 -> x2, blocking collectives: 78.7 us -> 140 us  [the longest x1 132 us: body(): lax.psum((plus_part, minus_part), 'doc')]
where the time goes in v1:
time: 382 us; the launch traced here: 380 us
  blocking collectives  152 us (40%)
  waiting for transfers between devices  148 us (39%)
  matrix products  48.7 us (13%)
  local copies, waits for them, and re-layouts  14.2 us (4%)
  between operations  14.2 us (4%)
    reduce_scatter x1, waiting for transfers between devices, body(): lax.psum_scatter(feature_hist(bins, weights), 'doc', scatter_dimension=0,...  148 us
    psum x1, blocking collectives, body(): lax.psum((plus_part, minus_part), 'doc')  132 us
    dot_general x16, matrix products, block_hist(): jnp.einsum('gr,nbr->ngb', weights, one_hot, preferred_element_type=jnp.fl...  48.7 us
    eq x16, local copies, waits for them, and re-layouts, block_hist(): bin_rows[:, None, :] == levels[None, :, None]  12.8 us
    all_gather x1, blocking collectives, body(): gradients = lax.all_gather(own_rows, 'feat', axis=1, tiled=True)  11.2 us
    psum x1, blocking collectives, body(): lax.psum(lax.psum((plus_part, minus_part), 'doc'), 'feat')  8.6 us
  transfers between devices with their start and end apart: 1, of which 1 were waited for; matrix products, arithmetic and copies ran while one was open for 0% of the time, Pallas kernels for 0%

profile of v1, /device:TPU:2, one launch (start us, length us, event | category | flops | bytes accessed | tf_op | source)
XLA Modules:
  0.0 380.5 jit_solution(9128182956396670990)
XLA Ops:
  8.1 0.9 fusion.26
  9.2 1.0 divide_reduce_fusion
  10.2 131.8 %all-reduce = (f32[128]{0:T(128)S(1)}, f32[128]{0:T(128)S(1)}) all-reduce(f32[128]{0:T(128)S(1)} %get-tuple-element.47, f32[128]{0:T(128)S(1)} %get-tuple-element.46), channel_id=1, replica_groups=mesh['doc'=64,'feat'=4] {'doc'}, use_global_device_ids=true, to_apply=%region_3.4 | all-reduce | flops 256 | bytes 2048 | tf_op jit(solution)/shard_map/psum | solution.py:85
  141.9 8.6 %all-reduce.1 = (f32[128]{0:T(128)S(1)}, f32[128]{0:T(128)S(1)}) all-reduce(f32[128]{0:T(128)S(1)} %get-tuple-element.58, f32[128]{0:T(128)S(1)} %get-tuple-element.59), channel_id=1, replica_groups=mesh['doc'=64,'feat'=4] {'feat'}, use_global_device_ids=true, to_apply=%region_4.5 | all-reduce | flops 256 | bytes 2048 | tf_op jit(solution)/shard_map/psum | solution.py:85
  151.2 11.2 %all_gather.3 = f32[2,1536]{1,0:T(2,128)S(1)} all-gather(f32[2,384]{1,0:T(2,128)S(1)} %pad_maximum_fusion.1), channel_id=1, replica_groups=mesh['doc'=64,'feat'=4] {'feat'}, dimensions={1}, use_global_device_ids=true | all-gather | bytes 15360 | tf_op jit(solution)/shard_map/all_gather | solution.py:87
  163.2 61.6 %while.11 = (s32[]{:T(128)}, f32[16,8,64,256]{3,2,1,0:T(8,128)}, s32[16,8,1536]{2,1,0:T(8,128)}, bf16[64,1536]{1,0:T(8,128)(2,1)S(1)}, s32[]{:T(128)}) while((s32[]{:T(128)}, f32[16,8,64,256]{3,2,1,0:T(8,128)}, s32[16,8,1536]{2,1,0:T(8,128)}, bf16[64,1536]{1,0:T(8,128)(2,1)S(1)}, s32[]{:T(128)}) %tuple.41), condition=%wide.region_13.14_spmd.clone, body=%wide.region_12.13_spmd.clone.sunk | while | flops 405798912 | bytes 868929 | solution.py:70
  163.2 0.8 dynamic-slice_bitcast_fusion.2
  164.0 3.0 fusion.31
  167.0 0.8 dynamic-slice_bitcast_fusion.2
  167.8 3.1 fusion.31
  170.9 0.8 dynamic-slice_bitcast_fusion.2
  171.7 3.1 fusion.31
  174.8 0.8 dynamic-slice_bitcast_fusion.2
  175.6 3.1 fusion.31
  178.6 0.8 dynamic-slice_bitcast_fusion.2
  179.4 3.0 fusion.31
  182.4 0.8 dynamic-slice_bitcast_fusion.2
  183.2 3.1 fusion.31
  187.1 3.0 fusion.31
  190.1 0.8 dynamic-slice_bitcast_fusion.2
  190.9 3.1 fusion.31
  194.0 0.8 dynamic-slice_bitcast_fusion.2
  194.8 3.0 fusion.31
  197.8 0.8 dynamic-slice_bitcast_fusion.2
  198.6 3.1 fusion.31
  202.5 3.0 fusion.31
  206.3 3.1 fusion.31
  210.2 3.0 fusion.31
  214.0 3.1 fusion.31
  217.9 3.0 fusion.31
  221.7 3.1 fusion.31
  224.8 148.2 %reduce-scatter.2.cloned.1.call-done = f32[2,64,256]{2,1,0:T(8,128)} async-done(((f32[128,64,256]{2,1,0:T(8,128)}), f32[2,64,256]{2,1,0:T(8,128)}) %reduce-scatter.2.cloned.1.call-update) | async-done | bytes 131088 | tf_op jit(solution)/shard_map/reduce_scatter | solution.py:90
  (34 shorter events, 8.6 us)
Async XLA Ops:
  7.2 365.9 %reduce-scatter.2.cloned.1.call-start = ((), (), s32[]{:S(2)}) async-start(), calls=%async_computation.1 | async-start | bytes 8519680 | tf_op jit(solution)/shard_map/reduce_scatter | solution.py:90
  150.6 12.6 %copy-start = (f32[128]{0:T(128)}, f32[128]{0:T(128)S(1)}, u32[]{:S(2)}) copy-start(f32[128]{0:T(128)S(1)} %divide_sqrt_fusion) | copy-start | bytes 1540
  150.7 12.5 %copy-start.1 = (f32[128]{0:T(128)}, f32[128]{0:T(128)S(1)}, u32[]{:S(2)}) copy-start(f32[128]{0:T(128)S(1)} %divide_sqrt_fusion.1) | copy-start | bytes 1540
Sparse Core Ops, SparseCore 0:
  224.9 148.0 reduce-scatter.1
